TPU v7x, 128 devices: a whole 4x4x4 slice. The times are simulated.
128 devices in a mesh: row: 8 (over x, z_hi), col: 16 (over y, z_lo, core).
Axes of the slice: x: 4, y: 4, z: 4 (z_hi: 2, z_lo: 2; z = z_hi * 2 + z_lo), core: 2. Of those that a mesh axis runs over, the one named last changes fastest.
Arguments:
- points: float32 [8, 131072], P(None, ('row', 'col')), may hold values from -4 to 4
- point_order: int32 [128, 1024], P(('row', 'col')), may hold values from 0 to 1023, each once within a row
- noise_var: float32 [131072], P(('row', 'col')), may hold values from 0.1 to 3
- inv_scale: float32 [8], replicated, may hold values from 0.2 to 0.6
- basis_vectors: float32 [16, 64, 131072], P(None, None, ('row', 'col')), may hold values from -4 to 4
- current: float32 [64, 131072], P(None, ('row', 'col')), may hold values from -22 to 22
- tile_rows: int32 [8, 16, 64], P('row', 'col'), may hold values from 0 to 63, as said below
- tile_cols: int32 [8, 16, 64], P('row', 'col'), may hold values from 0 to 31
Outputs:
- lanczos_next: float32 [64, 131072], P(None, ('row', 'col'))
- coefficients: float32 [4, 64], replicated
- gradient_product: float32 [64, 131072], P(None, ('row', 'col'))
Inputs may be any that keep to these rules, and one draw needn't show every extreme that they name: In each grid cell the 64 pairs (tile_rows, tile_cols) are distinct; each cell lists its 4 pairs with I = J; over all cells no unordered pair of distinct blocks is listed twice: it is listed as (I, J) with I < J when I + J is odd and with I > J when I + J is even.
All inputs are finite; a program needn't handle non-finite values.
Results may differ from a plain program's by a relative error of at most 0.00019.
Values sent between devices are 32-bit elements; how exact they have to be, the bound alone decides.
No kernel may reach another device: no remote copies, remote signals or barrier semaphores. Data moves between devices by JAX's collectives and lax.ppermute only.
A program may use at most 128 MiB of HBM per device.

v0:
```python
import math
import jax
import jax.numpy as jnp
from jax import lax
from jax.sharding import PartitionSpec as P

BLOCK = 256
ITERS = 2
ROOT_THREE = math.sqrt(3.0)
SUPPORT = 3.0
EPSILON = 1e-06
HIGHEST = lax.Precision.HIGHEST


def kernel_tiles(row_points, col_points):
    dist_sq = jnp.zeros(
        (row_points.shape[1], row_points.shape[2], col_points.shape[2]), jnp.float32
    )
    for feature in range(row_points.shape[0]):
        differ = row_points[feature][:, :, None] - col_points[feature][:, None, :]
        dist_sq = dist_sq + differ * differ
    shifted = dist_sq + EPSILON
    radius = jnp.sqrt(shifted)
    decaying = jnp.exp(-ROOT_THREE * radius)
    matern_part = (1.0 + ROOT_THREE * radius) * decaying
    tapered = jnp.maximum(1.0 - radius / SUPPORT, 0.0)
    taper_cube = tapered * tapered * tapered
    weight = taper_cube * tapered * (1.0 + 4.0 * radius / SUPPORT)
    kernel_tile = matern_part * weight
    slope_tile = shifted * (
        3.0 * decaying * weight + 20.0 * matern_part * taper_cube / (SUPPORT * SUPPORT)
    )
    return (kernel_tile, slope_tile)


def tile_products(
    col_values, row_values, col_points, row_points, row_blocks, col_blocks, mirror_mask, with_slope
):
    probe_count = col_values.shape[0]
    block_len = col_values.shape[2]
    group_size = math.gcd(row_blocks.shape[0], 8)
    layers = 2 if with_slope else 1
    row_total = jnp.zeros((layers, probe_count, row_values.shape[1], block_len), jnp.float32)
    col_total = jnp.zeros((layers, probe_count, col_values.shape[1], block_len), jnp.float32)
    grouped = (
        row_blocks.reshape(-1, group_size),
        col_blocks.reshape(-1, group_size),
        mirror_mask.reshape(-1, group_size),
    )

    def one_group(carried, listed):
        row_acc, col_acc = carried
        row_pick, col_pick, mirror_pick = listed
        kernel_tile, slope_tile = kernel_tiles(
            jnp.take(row_points, row_pick, axis=1), jnp.take(col_points, col_pick, axis=1)
        )
        if with_slope:
            stacked = jnp.stack([kernel_tile, slope_tile])
        else:
            stacked = kernel_tile[None]
        col_side = jnp.take(col_values, col_pick, axis=1)
        row_side = jnp.take(row_values, row_pick, axis=1) * mirror_pick[None, :, None]
        direct = jnp.einsum("pgj,kgij->kpgi", col_side, stacked, precision=HIGHEST)
        mirrored = jnp.einsum("pgi,kgij->kpgj", row_side, stacked, precision=HIGHEST)
        return (
            (row_acc.at[:, :, row_pick].add(direct), col_acc.at[:, :, col_pick].add(mirrored)),
            None,
        )

    (row_total, col_total), unused = lax.scan(one_group, (row_total, col_total), grouped)
    return (
        row_total.reshape(layers * probe_count, -1),
        col_total.reshape(layers * probe_count, -1),
    )


def both_sides(stacked):
    col_side = lax.all_gather(stacked, "row", axis=1, tiled=True)
    row_side = lax.all_gather(stacked, "col", axis=1, tiled=True)
    return (col_side, row_side)


def reduce_parts(row_part, col_part):
    from_rows = lax.psum_scatter(row_part, "col", scatter_dimension=1, tiled=True)
    from_cols = lax.psum_scatter(col_part, "row", scatter_dimension=1, tiled=True)
    return from_rows + from_cols


def on_device(
    points, point_order, noise_var, inv_scale, basis_vectors, current, tile_rows, tile_cols
):
    feature_count = points.shape[0]
    probe_count = current.shape[0]
    per_device = points.shape[1]
    block_count = per_device // BLOCK
    row_count = lax.axis_size("row")
    col_count = lax.axis_size("col")
    point_total = per_device * row_count * col_count
    arrangement = point_order[0]
    scaled = jnp.take(points, arrangement, axis=1) * inv_scale[:, None]
    noise_here = jnp.take(noise_var, arrangement)
    row_blocks = tile_rows[0, 0]
    col_blocks = tile_cols[0, 0]
    global_row = lax.axis_index("row") * col_count * block_count + row_blocks
    global_col = (
        col_blocks // block_count * col_count + lax.axis_index("col")
    ) * block_count + col_blocks % block_count
    mirror_mask = (global_row != global_col).astype(jnp.float32)
    earlier = basis_vectors
    coefficient_rows = []
    gradient_product = current
    col_points = scaled
    row_points = scaled
    for iteration in range(ITERS):
        if iteration == 0:
            stacked = jnp.concatenate([scaled, current], axis=0)
            apply_col_side, apply_row_side = both_sides(stacked)
            apply_col_points = apply_col_side[:feature_count].reshape(feature_count, -1, BLOCK)
            apply_row_points = apply_row_side[:feature_count].reshape(feature_count, -1, BLOCK)
            apply_row_part, apply_col_part = tile_products(
                apply_col_side[feature_count:].reshape(probe_count, -1, BLOCK),
                apply_row_side[feature_count:].reshape(probe_count, -1, BLOCK),
                apply_col_points,
                apply_row_points,
                row_blocks,
                col_blocks,
                mirror_mask,
                True,
            )
            summed = reduce_parts(apply_row_part, apply_col_part)
            image_vec = summed[:probe_count] + noise_here * current
            gradient_product = summed[probe_count:]
            col_points = apply_col_points
            row_points = apply_row_points
        else:
            col_side, row_side = both_sides(current)
            row_part, col_part = tile_products(
                col_side.reshape(probe_count, -1, BLOCK),
                row_side.reshape(probe_count, -1, BLOCK),
                col_points,
                row_points,
                row_blocks,
                col_blocks,
                mirror_mask,
                False,
            )
            image_vec = reduce_parts(row_part, col_part) + noise_here * current
        earlier_dots, alpha_now = lax.psum(
            (
                jnp.einsum("hpn,pn->hp", earlier, image_vec, precision=HIGHEST),
                jnp.sum(current * image_vec, axis=1),
            ),
            ("row", "col"),
        )
        earlier_dots = earlier_dots / point_total
        alpha_now = alpha_now / point_total
        residual_vec = (
            image_vec
            - alpha_now[:, None] * current
            - jnp.einsum("hp,hpn->pn", earlier_dots, earlier, precision=HIGHEST)
        )
        residual_sq = (
            lax.psum(jnp.sum(residual_vec * residual_vec, axis=1), ("row", "col")) / point_total
        )
        beta_now = jnp.sqrt(residual_sq + EPSILON)
        coefficient_rows += [alpha_now, beta_now]
        if iteration + 1 < ITERS:
            earlier = jnp.concatenate([earlier, current[None]], axis=0)
        current = residual_vec / beta_now[:, None]
    return (current, jnp.stack(coefficient_rows), gradient_product)


def solution(mesh):
    return jax.shard_map(
        on_device,
        mesh=mesh,
        in_specs=(
            P(None, ("row", "col")),
            P(("row", "col"), None),
            P(("row", "col")),
            P(),
            P(None, None, ("row", "col")),
            P(None, ("row", "col")),
            P("row", "col", None),
            P("row", "col", None),
        ),
        out_specs=(P(None, ("row", "col")), P(), P(None, ("row", "col"))),
        check_vma=False,
    )
```

profile of v0, /device:TPU:1, one launch (start us, length us, event | category | flops | bytes accessed | tf_op | source)
XLA Modules:
  0.0 1346.3 jit_solution(8351384830638760810)
XLA Ops:
  17.7 55.4 %all-gather.7.cloned.1.call-done = f32[72,8192]{1,0:T(8,128)} async-done(((f32[72,1024]{1,0:T(8,128)}), f32[72,8192]{1,0:T(8,128)}) %all-gather.7.cloned.1.call-update) | async-done | bytes 2359312 | tf_op jit(solution)/shard_map/all_gather | solution.py:78
  76.3 36.9 %all-gather.5.cloned.1.call-done = f32[72,16384]{1,0:T(8,128)} async-done(((f32[72,1024]{1,0:T(8,128)}), f32[72,16384]{1,0:T(8,128)}) %all-gather.5.cloned.1.call-update) | async-done | bytes 4718608 | tf_op jit(solution)/shard_map/all_gather | solution.py:79
  127.0 261.6 %while.30 = (s32[]{:T(128)}, f32[2,64,64,256]{3,1,2,0:T(8,128)}, f32[2,64,32,256]{3,1,2,0:T(8,128)}, s32[8,8]{1,0:T(8,128)S(1)}, f32[8,64,256]{2,0,1:T(8,128)}, ...) while((s32[]{:T(128)}, f32[2,64,64,256]{3,1,2,0:T(8,128)}, ...), condition=%wide.region_3.8_spmd, body=%wide.region_0.7_spmd.sunk | while | flops 1637255296 | bytes 25305864 | solution.py:70
  129.6 5.7 fusion.113
  139.6 4.5 fusion.116
  150.4 5.9 fusion.114
  162.2 5.7 fusion.113
  172.2 4.5 fusion.116
  183.1 5.9 fusion.114
  195.0 5.7 fusion.113
  204.9 4.5 fusion.116
  215.7 5.9 fusion.114
  227.6 5.7 fusion.113
  237.6 4.5 fusion.116
  248.4 5.9 fusion.114
  260.3 5.7 fusion.113
  281.0 5.9 fusion.114
  292.9 5.7 fusion.113
  313.7 5.9 fusion.114
  325.6 5.7 fusion.113
  335.6 4.5 fusion.116
  346.4 5.9 fusion.114
  358.3 5.7 fusion.113
  379.1 5.9 fusion.114
  388.6 4.6 copy.34
  393.2 5.4 copy.88
  398.7 8.2 copy.33
  406.9 9.7 copy.87
  416.7 12.2 all-gather.9.cloned.1.call-start
  429.0 4.5 gather_fusion.9
  433.5 49.1 %reduce-scatter.7.cloned.1.call-done = f32[128,1024]{1,0:T(8,128)} async-done(((f32[128,8192]{1,0:T(8,128)}), f32[128,1024]{1,0:T(8,128)}) %reduce-scatter.7.cloned.1.call-update) | async-done | bytes 524304 | tf_op jit(solution)/shard_map/reduce_scatter | solution.py:85
  482.6 99.5 %reduce-scatter.5.cloned.1.call-done = f32[128,1024]{1,0:T(8,128)} async-done(((f32[128,16384]{1,0:T(8,128)}), f32[128,1024]{1,0:T(8,128)}) %reduce-scatter.5.cloned.1.call-update) | async-done | bytes 524304 | tf_op jit(solution)/shard_map/reduce_scatter | solution.py:84
  583.6 9.0 fusion.67
  592.5 65.6 %all-reduce.1 = (f32[16,64]{0,1:T(8,128)S(1)}, f32[64]{0:T(128)S(1)}) all-reduce(f32[16,64]{0,1:T(8,128)S(1)} %bitcast.438, f32[64]{0:T(128)S(1)} %get-tuple-element.445), channel_id=1, replica_groups=mesh['row'=8,'col'=16] {'row','col'}, use_global_device_ids=true, to_apply=%region_8.13 | all-reduce | flops 1088 | bytes 8704 | tf_op jit(solution)/shard_map/psum | solution.py:148
  658.2 6.5 fusion.65
  666.1 63.1 %psum.44 = f32[64]{0:T(128)S(1)} all-reduce(f32[64]{0:T(128)S(1)} %get-tuple-element.401), channel_id=1, replica_groups=mesh['row'=8,'col'=16] {'row','col'}, use_global_device_ids=true, to_apply=%region_10.15 | all-reduce | flops 64 | bytes 512 | tf_op jit(solution)/shard_map/psum | solution.py:163
  731.3 49.9 %all-gather.9.cloned.1.call-done = f32[64,8192]{1,0:T(8,128)} async-done(((f32[64,1024]{1,0:T(8,128)}), f32[64,8192]{1,0:T(8,128)}) %all-gather.9.cloned.1.call-update) | async-done | bytes 2097168 | tf_op jit(solution)/shard_map/all_gather | solution.py:78
  784.5 36.7 %all-gather.11.cloned.1.call-done = f32[64,16384]{1,0:T(8,128)} async-done(((f32[64,1024]{1,0:T(8,128)}), f32[64,16384]{1,0:T(8,128)}) %all-gather.11.cloned.1.call-update) | async-done | bytes 4194320 | tf_op jit(solution)/shard_map/all_gather | solution.py:79
  821.2 4.9 copy.177
  828.8 214.8 %while.31 = (s32[]{:T(128)}, f32[1,64,64,256]{3,1,2,0:T(8,128)}, f32[1,64,32,256]{3,1,2,0:T(8,128)S(1)}, s32[8,8]{1,0:T(8,128)S(1)}, f32[8,64,256]{2,0,1:T(8,128...) while((s32[]{:T(128)}, f32[1,64,64,256]{3,1,2,0:T(8,128)}, ...), condition=%wide.region_14.19_spmd, body=%wide.region_11.18_spmd.sunk | while | flops 845842560 | bytes 8660057 | solution.py:70
  835.0 7.2 convolution_bitcast_fusion.5
  845.9 7.0 convolution_bitcast_fusion.4
  861.8 7.2 convolution_bitcast_fusion.5
  872.8 7.0 convolution_bitcast_fusion.4
  888.7 7.2 convolution_bitcast_fusion.5
  899.7 7.0 convolution_bitcast_fusion.4
  915.5 7.2 convolution_bitcast_fusion.5
  926.5 7.0 convolution_bitcast_fusion.4
  942.4 7.2 convolution_bitcast_fusion.5
  953.3 7.0 convolution_bitcast_fusion.4
  969.2 7.2 convolution_bitcast_fusion.5
  980.2 7.0 convolution_bitcast_fusion.4
  996.1 7.2 convolution_bitcast_fusion.5
  1007.0 7.0 convolution_bitcast_fusion.4
  1022.9 7.2 convolution_bitcast_fusion.5
  1033.9 7.0 convolution_bitcast_fusion.4
  1045.4 4.6 copy.89
  1051.0 4.9 pad_maximum_fusion.7
  1056.0 64.1 %reduce-scatter.11.cloned.1.call-done = f32[64,1024]{1,0:T(8,128)} async-done(((f32[64,8192]{1,0:T(8,128)}), f32[64,1024]{1,0:T(8,128)}) %reduce-scatter.11.cloned.1.call-update) | async-done | bytes 262160 | tf_op jit(solution)/shard_map/reduce_scatter | solution.py:85
  1120.1 67.1 %reduce-scatter.9.cloned.1.call-done = f32[64,1024]{1,0:T(8,128)} async-done(((f32[64,16384]{1,0:T(8,128)}), f32[64,1024]{1,0:T(8,128)}) %reduce-scatter.9.cloned.1.call-update) | async-done | bytes 262160 | tf_op jit(solution)/shard_map/reduce_scatter | solution.py:84
  1188.5 10.2 fusion.63
  1198.7 68.3 %all-reduce = (f32[17,64]{0,1:T(8,128)S(1)}, f32[64]{0:T(128)S(1)}) all-reduce(f32[17,64]{0,1:T(8,128)S(1)} %bitcast.439, f32[64]{0:T(128)S(1)} %get-tuple-element.399), channel_id=1, replica_groups=mesh['row'=8,'col'=16] {'row','col'}, use_global_device_ids=true, to_apply=%region_19.24 | all-reduce | flops 1152 | bytes 9216 | tf_op jit(solution)/shard_map/psum | solution.py:148
  1267.0 7.8 fusion.61
  1275.1 62.6 %psum.47 = f32[64]{0:T(128)S(1)} all-reduce(f32[64]{0:T(128)S(1)} %get-tuple-element.397), channel_id=1, replica_groups=mesh['row'=8,'col'=16] {'row','col'}, use_global_device_ids=true, to_apply=%region_21.26 | all-reduce | flops 64 | bytes 512 | tf_op jit(solution)/shard_map/psum | solution.py:163
  (653 shorter events, 287.5 us)
Async XLA Ops:
  7.2 421.8 %copy-start = (f32[1024]{0:T(1024)S(1)}, f32[1024]{0:T(1024)}, u32[]{:S(2)}) copy-start(f32[1024]{0:T(1024)} %param.22) | copy-start | bytes 12292
  7.2 6.3 copy-start.4
  7.2 8.4 copy-start.18
  7.2 9.1 copy-start.19
  7.2 65.9 %all-gather.7.cloned.1.call-start = ((), (), s32[]{:S(2)}) async-start(), calls=%async_computation.5 | async-start | bytes 2654208 | tf_op jit(solution)/shard_map/all_gather | solution.py:78
  14.3 98.8 %all-gather.5.cloned.1.call-start = ((), (), s32[]{:S(2)}) async-start(), calls=%async_computation.4 | async-start | bytes 5013504 | tf_op jit(solution)/shard_map/all_gather | solution.py:79
  15.0 467.6 %reduce-scatter.7.cloned.1.call-start = ((), (), s32[]{:S(2)}) async-start(), calls=%async_computation.7 | async-start | bytes 4718592 | tf_op jit(solution)/shard_map/reduce_scatter | solution.py:85
  73.1 1.6 slice-start
  124.5 2.5 slice-start.1
  398.6 183.5 %reduce-scatter.5.cloned.1.call-start = ((), (), s32[]{:S(2)}) async-start(), calls=%async_computation.6 | async-start | bytes 8912896 | tf_op jit(solution)/shard_map/reduce_scatter | solution.py:84
  416.7 16.8 %copy-start.13 = (s32[1,1024]{1,0:T(1,128)S(1)}, s32[1,1024]{1,0:T(1,128)}, u32[]{:S(2)}) copy-start(s32[1,1024]{1,0:T(1,128)} %param.21) | copy-start | bytes 12292
  416.7 166.7 %copy-start.5 = (f32[64,1024]{1,0:T(8,128)S(1)}, f32[64,1024]{1,0:T(8,128)}, u32[]{:S(2)}) copy-start(f32[64,1024]{1,0:T(8,128)} %param.25) | copy-start | bytes 786436
  416.7 364.5 %all-gather.9.cloned.1.call-start = ((), (), s32[]{:S(2)}) async-start(), calls=%async_computation.8 | async-start | bytes 2359296 | tf_op jit(solution)/shard_map/all_gather | solution.py:78
  433.5 231.7 %copy-start.7 = (f32[1,1024]{1,0:T(1,128)}, f32[1,1024]{1,0:T(1,128)S(1)}, u32[]{:S(2)}) copy-start(f32[1,1024]{1,0:T(1,128)S(1)} %and_select_fusion) | copy-start | bytes 12292
  666.1 118.4 %copy-start.2 = (f32[64,1024]{1,0:T(8,128)}, f32[64,1024]{1,0:T(8,128)S(1)}, u32[]{:S(2)}) copy-start(f32[64,1024]{1,0:T(8,128)S(1)} %get-tuple-element.402) | copy-start | bytes 786436
  729.8 54.6 %copy-start.14 = (f32[64]{0:T(128)}, f32[64]{0:T(128)S(1)}, u32[]{:S(2)}) copy-start(f32[64]{0:T(128)S(1)} %get-tuple-element.451) | copy-start | bytes 772
  730.6 90.6 %all-gather.11.cloned.1.call-start = ((), (), s32[]{:S(2)}) async-start(), calls=%async_computation.9 | async-start | bytes 4456448 | tf_op jit(solution)/shard_map/all_gather | solution.py:79
  731.2 388.9 %reduce-scatter.11.cloned.1.call-start = ((), (), s32[]{:S(2)}) async-start(), calls=%async_computation.11 | async-start | bytes 2359296 | tf_op jit(solution)/shard_map/reduce_scatter | solution.py:85
  828.9 1.8 copy-start.11
  828.9 2.6 copy-start.9
  842.7 3.2 copy-start.10
  845.9 7.0 copy-start.12
  855.7 1.8 copy-start.11
  855.7 2.6 copy-start.9
  869.5 3.2 copy-start.10
  872.8 7.0 copy-start.12
  882.6 1.8 copy-start.11
  882.6 2.6 copy-start.9
  896.4 3.2 copy-start.10
  899.6 7.0 copy-start.12
  909.4 1.8 copy-start.11
  909.4 2.6 copy-start.9
  923.3 3.2 copy-start.10
  926.5 7.0 copy-start.12
  936.2 1.8 copy-start.11
  936.3 2.6 copy-start.9
  950.1 3.2 copy-start.10
  953.3 7.0 copy-start.12
  963.1 1.8 copy-start.11
  963.1 2.6 copy-start.9
  976.9 3.2 copy-start.10
  980.2 7.0 copy-start.12
  989.9 1.8 copy-start.11
  989.9 2.6 copy-start.9
  1003.8 3.2 copy-start.10
  1007.0 7.0 copy-start.12
  1016.8 1.8 copy-start.11
  1016.8 2.6 copy-start.9
  1030.6 3.2 copy-start.10
  1033.9 7.0 copy-start.12
  1045.2 142.1 %reduce-scatter.9.cloned.1.call-start = ((), (), s32[]{:S(2)}) async-start(), calls=%async_computation.10 | async-start | bytes 4456448 | tf_op jit(solution)/shard_map/reduce_scatter | solution.py:84
  1050.1 0.9 copy-start.6
  1051.0 136.2 %copy-start.3 = (f32[64,1024]{1,0:T(8,128)S(1)}, f32[64,1024]{1,0:T(8,128)}, u32[]{:S(2)}) copy-start(f32[64,1024]{1,0:T(8,128)} %copy-done.2) | copy-start | bytes 786436
  1051.0 136.2 %copy-start.8 = (f32[1,1024]{1,0:T(1,128)S(1)}, f32[1,1024]{1,0:T(1,128)}, u32[]{:S(2)}) copy-start(f32[1,1024]{1,0:T(1,128)} %copy-done.7) | copy-start | bytes 12292
  1051.0 136.2 %copy-start.15 = (f32[64]{0:T(128)S(1)}, f32[64]{0:T(128)}, u32[]{:S(2)}) copy-start(f32[64]{0:T(128)} %copy-done.14) | copy-start | bytes 772
  1267.0 71.6 %copy-start.16 = (f32[1,64]{1,0:T(1,128)S(1)}, f32[1,64]{1,0:T(1,128)}, u32[]{:S(2)}) copy-start(f32[1,64]{1,0:T(1,128)} %get-tuple-element.448) | copy-start | bytes 772
  1267.0 71.6 %copy-start.17 = (f32[1,64]{1,0:T(1,128)S(1)}, f32[1,64]{1,0:T(1,128)}, u32[]{:S(2)}) copy-start(f32[1,64]{1,0:T(1,128)} %get-tuple-element.450) | copy-start | bytes 772
  1267.0 72.1 %copy-start.1 = (f32[1024]{0:T(1024)S(1)}, f32[1024]{0:T(1024)}, u32[]{:S(2)}) copy-start(f32[1024]{0:T(1024)} %param.22) | copy-start | bytes 12292
Sparse Core Ops, SparseCore 0:
  14.4 58.6 all-gather.6
  74.7 38.3 all-gather.4
  398.8 83.8 reduce-scatter.6
  484.9 97.2 reduce-scatter.4
  730.8 50.4 all-gather.8
  783.3 37.8 all-gather.10
  1045.3 74.7 reduce-scatter.10
  1122.5 64.6 reduce-scatter.8
where the time goes:
time: 1360 us; the launch traced here: 1350 us
  waiting for transfers between devices  460 us (34%)
  blocking collectives  260 us (19%)
  matrix products  230 us (17%)
  local copies, waits for them, and re-layouts  212 us (16%)
  other arithmetic  153 us (11%)
  between operations  14.8 us (1%)
    reduce_scatter x2, waiting for transfers between devices, reduce_parts(): lax.psum_scatter(row_part, 'col', scatter_dimension=1, tiled=True)  167 us
    psum x2, blocking collectives, on_device(): lax.psum((jnp.einsum('hpn,pn->hp', earlier, image_vec, precision=HIGHEST)...  134 us
    psum x2, blocking collectives, on_device(): lax.psum(jnp.sum(residual_vec * residual_vec, axis=1), ('row', 'col'))  126 us
    reduce_scatter x2, waiting for transfers between devices, reduce_parts(): lax.psum_scatter(col_part, 'row', scatter_dimension=1, tiled=True)  113 us
    all_gather x2, waiting for transfers between devices, both_sides(): col_side = lax.all_gather(stacked, 'row', axis=1, tiled=True)  105 us
    dot_general x16, matrix products, one_group(): direct = jnp.einsum('pgj,kgij->kpgi', col_side, stacked, precision=HIGHEST)  103 us
    dot_general x16, matrix products, one_group(): jnp.einsum('pgi,kgij->kpgj', row_side, stacked, precision=HIGHEST)  93.6 us
    all_gather x2, waiting for transfers between devices, both_sides(): row_side = lax.all_gather(stacked, 'col', axis=1, tiled=True)  73.6 us
  transfers between devices with their start and end apart: 8, of which 8 were waited for; matrix products, arithmetic and copies ran while one was open for 3% of the time, Pallas kernels for 0%

commit v1 on v0

--- a/solution.py
+++ b/solution.py
@@ -75,7 +75,10 @@
 
 
 def both_sides(stacked):
-    col_side = lax.all_gather(stacked, "row", axis=1, tiled=True)
+    count = lax.axis_size("row")
+    blocks = jnp.stack([stacked for _ in range(count)])
+    blocks = lax.all_to_all(blocks, "row", split_axis=0, concat_axis=0)
+    col_side = jnp.concatenate(blocks, axis=1)
     row_side = lax.all_gather(stacked, "col", axis=1, tiled=True)
     return (col_side, row_side)
 

time: 1360 us -> 1280 us (0.941)
  waiting for transfers between devices: 460 us -> 347 us
  blocking collectives: 260 us -> 295 us
    all_gather x2 -> x0, waiting for transfers between devices: 105 us -> none  [both_sides(): col_side = lax.all_gather(stacked, 'row', axis=1, tiled=True)]
    all_gather x2, waiting for transfers between devices: 73.6 us -> 21.4 us  [both_sides(): row_side = lax.all_gather(stacked, 'col', axis=1, tiled=True)]
    all_to_all x0 -> x1, blocking collectives: none -> 35.4 us  [both_sides(): blocks = lax.all_to_all(blocks, 'row', split_axis=0, concat_axis=0)]
    all_to_all x0 -> x1, waiting for transfers between devices: none -> 32.2 us  [both_sides(): blocks = lax.all_to_all(blocks, 'row', split_axis=0, concat_axis=0)]
    gather x16, local copies, waits for them, and re-layouts: 25.5 us -> 8.88 us  [one_group(): jnp.take(row_points, row_pick, axis=1)]
    gather x16, local copies, waits for them, and re-layouts: 8.88 us -> 24 us  [one_group(): jnp.take(col_points, col_pick, axis=1)]
  transfers between devices with their start and end apart: 8 -> 7, of which waited for: 8 -> 7; matrix products, arithmetic and copies ran while one was open for 3% -> 4% of each run, Pallas kernels for 0% -> 0%
where the time goes in v1:
time: 1280 us; the launch traced here: 1270 us
  waiting for transfers between devices  347 us (27%)
  blocking collectives  295 us (23%)
  matrix products  231 us (18%)
  local copies, waits for them, and re-layouts  216 us (17%)
  other arithmetic  154 us (12%)
  between operations  14.6 us (1%)
    reduce_scatter x2, waiting for transfers between devices, reduce_parts(): lax.psum_scatter(row_part, 'col', scatter_dimension=1, tiled=True)  167 us
    psum x2, blocking collectives, on_device(): lax.psum((jnp.einsum('hpn,pn->hp', earlier, image_vec, precision=HIGHEST)...  134 us
    reduce_scatter x2, waiting for transfers between devices, reduce_parts(): lax.psum_scatter(col_part, 'row', scatter_dimension=1, tiled=True)  127 us
    psum x2, blocking collectives, on_device(): lax.psum(jnp.sum(residual_vec * residual_vec, axis=1), ('row', 'col'))  126 us
    dot_general x16, matrix products, one_group(): direct = jnp.einsum('pgj,kgij->kpgi', col_side, stacked, precision=HIGHEST)  103 us
    dot_general x16, matrix products, one_group(): jnp.einsum('pgi,kgij->kpgj', row_side, stacked, precision=HIGHEST)  93.7 us
    gather x16, local copies, waits for them, and re-layouts, one_group(): jnp.take(row_values, row_pick, axis=1) * mirror_pick[None, :, None]  50.6 us
    scatter-add x16, other arithmetic, one_group(): row_acc.at[:, :, row_pick].add(direct)  48.4 us
  transfers between devices with their start and end apart: 7, of which 7 were waited for; matrix products, arithmetic and copies ran while one was open for 4% of the time, Pallas kernels for 0%

profile of v1, /device:TPU:1, one launch (start us, length us, event | category | flops | bytes accessed | tf_op | source)
XLA Modules:
  0.0 1270.0 jit_solution(4878872235146117051)
XLA Ops:
  16.9 8.3 all-to-all-start
  27.3 32.2 %all-to-all-done = f32[8,72,1024]{2,1,0:T(8,128)S(1)} async-done(((f32[8,72,1024]{2,1,0:T(8,128)}), f32[8,72,1024]{2,1,0:T(8,128)S(1)}, u32[]{:S(2)}, u32[]{:S(2)}) %all-to-all-start) | async-done | bytes 2359328 | tf_op jit(solution)/shard_map/all_to_all | solution.py:80
  67.8 11.4 all-gather.3.cloned.1.call-done
  91.0 255.9 %while.30 = (s32[]{:T(128)}, f32[2,64,64,256]{3,1,2,0:T(8,128)}, f32[2,64,32,256]{3,1,2,0:T(8,128)}, s32[8,8]{1,0:T(8,128)S(1)}, f32[8,64,256]{2,0,1:T(8,128)S(1...) while((s32[]{:T(128)}, f32[2,64,64,256]{3,1,2,0:T(8,128)}, ...), condition=%wide.region_3.8_spmd, body=%wide.region_0.7_spmd.sunk | while | flops 1637255296 | bytes 29500224 | solution.py:70
  93.6 5.7 fusion.113
  102.9 4.5 fusion.116
  113.7 5.9 fusion.114
  125.4 5.7 fusion.113
  134.7 4.5 fusion.116
  145.6 5.9 fusion.114
  157.4 5.7 fusion.113
  166.7 4.5 fusion.116
  177.5 5.9 fusion.114
  189.3 5.7 fusion.113
  198.6 4.5 fusion.116
  209.4 5.9 fusion.114
  221.2 5.7 fusion.113
  241.4 5.9 fusion.114
  253.2 5.7 fusion.113
  262.5 4.5 fusion.116
  273.4 5.9 fusion.114
  285.2 5.7 fusion.113
  305.3 5.9 fusion.114
  317.1 5.7 fusion.113
  337.3 5.9 fusion.114
  346.9 4.8 copy.58
  351.7 5.3 copy.112
  357.1 8.2 copy.57
  365.3 9.7 copy.111
  375.3 4.5 gather_fusion.9
  379.9 61.3 %reduce-scatter.7.cloned.1.call-done = f32[128,1024]{1,0:T(8,128)} async-done(((f32[128,8192]{1,0:T(8,128)}), f32[128,1024]{1,0:T(8,128)}) %reduce-scatter.7.cloned.1.call-update) | async-done | bytes 524304 | tf_op jit(solution)/shard_map/reduce_scatter | solution.py:88
  441.2 99.7 %reduce-scatter.5.cloned.1.call-done = f32[128,1024]{1,0:T(8,128)} async-done(((f32[128,16384]{1,0:T(8,128)}), f32[128,1024]{1,0:T(8,128)}) %reduce-scatter.5.cloned.1.call-update) | async-done | bytes 524304 | tf_op jit(solution)/shard_map/reduce_scatter | solution.py:87
  542.3 9.0 fusion.67
  551.3 65.7 %all-reduce.1 = (f32[16,64]{0,1:T(8,128)S(1)}, f32[64]{0:T(128)S(1)}) all-reduce(f32[16,64]{0,1:T(8,128)S(1)} %bitcast.432, f32[64]{0:T(128)S(1)} %get-tuple-element.485), channel_id=1, replica_groups=mesh['row'=8,'col'=16] {'row','col'}, use_global_device_ids=true, to_apply=%region_8.13 | all-reduce | flops 1088 | bytes 8704 | tf_op jit(solution)/shard_map/psum | solution.py:151
  617.0 6.5 fusion.65
  625.0 63.0 %psum.44 = f32[64]{0:T(128)S(1)} all-reduce(f32[64]{0:T(128)S(1)} %get-tuple-element.441), channel_id=1, replica_groups=mesh['row'=8,'col'=16] {'row','col'}, use_global_device_ids=true, to_apply=%region_10.15 | all-reduce | flops 64 | bytes 512 | tf_op jit(solution)/shard_map/psum | solution.py:166
  690.7 35.4 %all_to_all.10 = f32[8,64,1024]{2,1,0:T(8,128)S(1)} all-to-all(f32[8,64,1024]{2,1,0:T(8,128)S(1)} %stack.24), channel_id=1, replica_groups=mesh['row'=8,'col'=16] {'row'}, dimensions={0} | all-to-all | bytes 4194304 | tf_op jit(solution)/shard_map/all_to_all | solution.py:80
  733.2 10.0 all-gather.5.cloned.1.call-done
  743.1 4.8 copy.199
  751.4 215.1 %while.31 = (s32[]{:T(128)}, f32[1,64,64,256]{3,1,2,0:T(8,128)}, f32[1,64,32,256]{3,1,2,0:T(8,128)S(1)}, s32[8,8]{1,0:T(8,128)S(1)}, f32[8,64,256]{2,0,1:T(8,128...) while((s32[]{:T(128)}, f32[1,64,64,256]{3,1,2,0:T(8,128)}, ...), condition=%wide.region_14.19_spmd, body=%wide.region_11.18_spmd.sunk | while | flops 845842560 | bytes 10759349 | solution.py:70
  757.5 7.2 convolution_bitcast_fusion.5
  768.6 7.0 convolution_bitcast_fusion.4
  784.4 7.2 convolution_bitcast_fusion.5
  795.4 7.0 convolution_bitcast_fusion.4
  811.3 7.2 convolution_bitcast_fusion.5
  822.4 7.0 convolution_bitcast_fusion.4
  838.2 7.2 convolution_bitcast_fusion.5
  849.3 7.0 convolution_bitcast_fusion.4
  865.1 7.2 convolution_bitcast_fusion.5
  876.1 7.0 convolution_bitcast_fusion.4
  891.9 7.2 convolution_bitcast_fusion.5
  903.0 7.0 convolution_bitcast_fusion.4
  918.8 7.2 convolution_bitcast_fusion.5
  929.9 7.0 convolution_bitcast_fusion.4
  945.7 7.2 convolution_bitcast_fusion.5
  956.8 7.0 convolution_bitcast_fusion.4
  968.1 4.6 copy.113
  973.7 4.9 pad_maximum_fusion.7
  978.6 65.2 %reduce-scatter.11.cloned.1.call-done = f32[64,1024]{1,0:T(8,128)} async-done(((f32[64,8192]{1,0:T(8,128)}), f32[64,1024]{1,0:T(8,128)}) %reduce-scatter.11.cloned.1.call-update) | async-done | bytes 262160 | tf_op jit(solution)/shard_map/reduce_scatter | solution.py:88
  1043.8 66.9 %reduce-scatter.9.cloned.1.call-done = f32[64,1024]{1,0:T(8,128)} async-done(((f32[64,16384]{1,0:T(8,128)}), f32[64,1024]{1,0:T(8,128)}) %reduce-scatter.9.cloned.1.call-update) | async-done | bytes 262160 | tf_op jit(solution)/shard_map/reduce_scatter | solution.py:87
  1112.0 10.2 fusion.63
  1122.2 68.5 %all-reduce = (f32[17,64]{0,1:T(8,128)S(1)}, f32[64]{0:T(128)S(1)}) all-reduce(f32[17,64]{0,1:T(8,128)S(1)} %bitcast.433, f32[64]{0:T(128)S(1)} %get-tuple-element.439), channel_id=1, replica_groups=mesh['row'=8,'col'=16] {'row','col'}, use_global_device_ids=true, to_apply=%region_19.24 | all-reduce | flops 1152 | bytes 9216 | tf_op jit(solution)/shard_map/psum | solution.py:151
  1190.8 7.8 fusion.61
  1198.9 62.6 %psum.47 = f32[64]{0:T(128)S(1)} all-reduce(f32[64]{0:T(128)S(1)} %get-tuple-element.437), channel_id=1, replica_groups=mesh['row'=8,'col'=16] {'row','col'}, use_global_device_ids=true, to_apply=%region_21.26 | all-reduce | flops 64 | bytes 512 | tf_op jit(solution)/shard_map/psum | solution.py:166
  (735 shorter events, 290.8 us)
Async XLA Ops:
  7.2 368.1 %copy-start = (f32[1024]{0:T(1024)S(1)}, f32[1024]{0:T(1024)}, u32[]{:S(2)}) copy-start(f32[1024]{0:T(1024)} %param.22) | copy-start | bytes 12292
  7.2 6.3 copy-start.7
  7.2 72.0 %all-gather.3.cloned.1.call-start = ((), (), s32[]{:S(2)}) async-start(), calls=%async_computation.6 | async-start | bytes 5013504 | tf_op jit(solution)/shard_map/all_gather | solution.py:82
  16.9 8.8 copy-start.23
  16.9 9.6 copy-start.24
  16.9 42.6 %all-to-all-start = ((f32[8,72,1024]{2,1,0:T(8,128)}), f32[8,72,1024]{2,1,0:T(8,128)S(1)}, u32[]{:S(2)}, u32[]{:S(2)}) async-start(f32[8,72,1024]{2,1,0:T(8,128)} %stack.23), calls=%async_computation | async-start | bytes 4718592 | tf_op jit(solution)/shard_map/all_to_all | solution.py:80
  25.2 416.0 %reduce-scatter.7.cloned.1.call-start = ((), (), s32[]{:S(2)}) async-start(), calls=%async_computation.8 | async-start | bytes 4718592 | tf_op jit(solution)/shard_map/reduce_scatter | solution.py:88
  91.0 2.5 copy-start.2
  119.6 3.3 copy-start.3
  122.9 2.5 copy-start.2
  151.5 3.4 copy-start.3
  154.9 2.5 copy-start.2
  183.4 3.3 copy-start.3
  215.3 3.3 copy-start.3
  247.3 3.3 copy-start.3
  279.3 3.3 copy-start.3
  311.2 3.4 copy-start.3
  343.2 3.3 copy-start.3
  346.9 4.8 copy-start.4
  357.0 183.9 %reduce-scatter.5.cloned.1.call-start = ((), (), s32[]{:S(2)}) async-start(), calls=%async_computation.7 | async-start | bytes 8912896 | tf_op jit(solution)/shard_map/reduce_scatter | solution.py:87
  375.1 4.8 copy-start.16
  375.1 368.1 %all-gather.5.cloned.1.call-start = ((), (), s32[]{:S(2)}) async-start(), calls=%async_computation.9 | async-start | bytes 4456448 | tf_op jit(solution)/shard_map/all_gather | solution.py:82
  379.9 244.2 %copy-start.10 = (f32[1,1024]{1,0:T(1,128)}, f32[1,1024]{1,0:T(1,128)S(1)}, u32[]{:S(2)}) copy-start(f32[1,1024]{1,0:T(1,128)S(1)} %and_select_fusion) | copy-start | bytes 12292
  617.0 7.1 copy-start.8
  688.6 37.5 %copy-start.17 = (f32[64]{0:T(128)}, f32[64]{0:T(128)S(1)}, u32[]{:S(2)}) copy-start(f32[64]{0:T(128)S(1)} %get-tuple-element.491) | copy-start | bytes 772
  689.4 354.4 %reduce-scatter.11.cloned.1.call-start = ((), (), s32[]{:S(2)}) async-start(), calls=%async_computation.11 | async-start | bytes 2359296 | tf_op jit(solution)/shard_map/reduce_scatter | solution.py:88
  765.3 3.2 copy-start.13
  768.5 7.1 copy-start.15
  775.6 2.7 copy-start.6
  775.6 2.7 copy-start.20
  792.2 3.2 copy-start.13
  795.4 7.1 copy-start.15
  802.5 2.8 copy-start.6
  802.5 2.8 copy-start.20
  819.1 3.2 copy-start.13
  822.4 7.1 copy-start.15
  829.4 2.7 copy-start.6
  829.4 2.7 copy-start.20
  846.0 3.2 copy-start.13
  849.2 7.0 copy-start.15
  856.3 2.7 copy-start.6
  856.3 2.7 copy-start.20
  872.9 3.2 copy-start.13
  876.1 7.0 copy-start.15
  883.1 2.8 copy-start.6
  883.1 2.8 copy-start.20
  899.8 3.2 copy-start.13
  903.0 7.1 copy-start.15
  910.0 2.7 copy-start.6
  910.0 2.7 copy-start.20
  926.7 3.2 copy-start.13
  929.9 7.0 copy-start.15
  936.9 2.7 copy-start.6
  936.9 2.7 copy-start.20
  953.5 3.2 copy-start.13
  956.8 7.0 copy-start.15
  963.8 2.8 copy-start.6
  963.8 2.8 copy-start.20
  968.1 142.6 %reduce-scatter.9.cloned.1.call-start = ((), (), s32[]{:S(2)}) async-start(), calls=%async_computation.10 | async-start | bytes 4456448 | tf_op jit(solution)/shard_map/reduce_scatter | solution.py:87
  973.7 137.0 %copy-start.11 = (f32[1,1024]{1,0:T(1,128)S(1)}, f32[1,1024]{1,0:T(1,128)}, u32[]{:S(2)}) copy-start(f32[1,1024]{1,0:T(1,128)} %copy-done.10) | copy-start | bytes 12292
  973.7 137.0 %copy-start.18 = (f32[64]{0:T(128)S(1)}, f32[64]{0:T(128)}, u32[]{:S(2)}) copy-start(f32[64]{0:T(128)} %copy-done.17) | copy-start | bytes 772
  1190.8 71.5 %copy-start.21 = (f32[1,64]{1,0:T(1,128)S(1)}, f32[1,64]{1,0:T(1,128)}, u32[]{:S(2)}) copy-start(f32[1,64]{1,0:T(1,128)} %get-tuple-element.488) | copy-start | bytes 772
  1190.8 71.5 %copy-start.22 = (f32[1,64]{1,0:T(1,128)S(1)}, f32[1,64]{1,0:T(1,128)}, u32[]{:S(2)}) copy-start(f32[1,64]{1,0:T(1,128)} %get-tuple-element.490) | copy-start | bytes 772
  1190.8 72.1 %copy-start.1 = (f32[1024]{0:T(1024)S(1)}, f32[1024]{0:T(1024)}, u32[]{:S(2)}) copy-start(f32[1024]{0:T(1024)} %param.22) | copy-start | bytes 12292
  (32 other events, 49.0 us)
Sparse Core Ops, SparseCore 0:
  14.4 64.7 all-gather.2
  357.2 84.0 reduce-scatter.6
  443.6 97.2 reduce-scatter.4
  689.5 53.5 all-gather.4
  968.2 75.5 reduce-scatter.10
  1046.1 64.6 reduce-scatter.8
